TPU v7x, 32 devices: a whole 2x2x4 slice. The times are simulated.
32 devices in a mesh: space: 8 (over z, x), freq: 4 (over y, core).
Axes of the slice: x: 2, y: 2, z: 4, core: 2. Of those that a mesh axis runs over, the one named last changes fastest.
Arguments:
- u_velocity: bfloat16 [2176, 16, 512], P(None, 'space', 'freq'), may hold values from -6 to 6
- v_velocity: bfloat16 [2176, 16, 512], P(None, 'space', 'freq'), may hold values from -6 to 6
- cell_weights: float32 [16, 512], P('space', 'freq'), may hold values from 0.25 to 4
- block_offsets: int32 [16], replicated, may hold values from 0 to 1920
- triads: int32 [64, 2], replicated, may hold values from 0 to 63
Outputs:
- eigen_values: float32 [64, 2], replicated
- mode_fields: float32 [64, 2, 16, 512], P(None, None, 'space', 'freq')
Inputs may be any that keep to these rules, and one draw needn't show every extreme that they name: `triads`: k and l are each below 64, so k + l is below 128.
All inputs are finite; a program needn't handle non-finite values.
Results may differ from a plain program's by a relative error of at most 0.012.
Values may be sent and summed in bfloat16 or wider, within the bound.
No kernel may reach another device: no remote copies, remote signals or barrier semaphores. Data moves between devices by JAX's collectives and lax.ppermute only.
A program may use at most 64 MiB of HBM per device.

v0:
```python
import math
import jax
import jax.numpy as jnp
from jax import lax
from jax.sharding import PartitionSpec as P

NFFT = 256
POW = 4


def with_halo(cells, sides, width):
    for axis, dim in sides:
        count = lax.axis_size(axis)
        ends = count - 1
        head = lax.slice_in_dim(cells, 0, width, axis=dim)
        tail = lax.slice_in_dim(cells, cells.shape[dim] - width, cells.shape[dim], axis=dim)
        cells = jnp.concatenate(
            [
                lax.ppermute(tail, axis, [(i, (i + 1) % count) for i in range(ends)]),
                cells,
                lax.ppermute(head, axis, [((i + 1) % count, i) for i in range(ends)]),
            ],
            axis=dim,
        )
    return cells


def make_table(length):
    half_len = length // 2
    times_idx = jnp.arange(length, dtype=jnp.int32)
    freq_idx = jnp.arange(half_len, dtype=jnp.int32)
    phases = freq_idx[:, None] * times_idx[None, :] % length
    angles = phases.astype(jnp.float32) * (2.0 * math.pi / length)
    window = 0.5 - 0.5 * jnp.cos(times_idx.astype(jnp.float32) * (2.0 * math.pi / length))
    scaling = 1.0 / jnp.sqrt(jnp.sum(window * window))
    transform = jnp.concatenate([jnp.cos(angles) * scaling, -jnp.sin(angles) * scaling], axis=0)
    return (window, transform.astype(jnp.bfloat16))


def spectra(vorticity, offsets):
    window, transform = make_table(NFFT)
    fluct = vorticity - jnp.mean(vorticity, axis=0, keepdims=True)
    blocks = jax.vmap(lambda start: lax.dynamic_slice_in_dim(fluct, start, NFFT, 0))(offsets)
    windowed = (blocks * window[None, :, None, None]).astype(jnp.bfloat16)
    return jnp.einsum("ft,btxy->bfxy", transform, windowed, preferred_element_type=jnp.float32)


def cross_terms(spectrum, weights, triads):
    half_len = spectrum.shape[1] // 2
    real_part = spectrum[:, :half_len]
    imag_part = spectrum[:, half_len:]
    target = triads[:, 0] + triads[:, 1]
    first_re = jnp.take(real_part, triads[:, 0], axis=1)
    first_im = jnp.take(imag_part, triads[:, 0], axis=1)
    second_re = jnp.take(real_part, triads[:, 1], axis=1)
    second_im = jnp.take(imag_part, triads[:, 1], axis=1)
    target_re = jnp.take(real_part, target, axis=1)
    target_im = jnp.take(imag_part, target, axis=1)
    prod_re = (first_re * second_re - first_im * second_im) * weights
    prod_im = (first_re * second_im + first_im * second_re) * weights
    high = lax.Precision.HIGHEST
    cross_re = jnp.einsum("btxy,ctxy->tbc", prod_re, target_re, precision=high) + jnp.einsum(
        "btxy,ctxy->tbc", prod_im, target_im, precision=high
    )
    cross_im = jnp.einsum("btxy,ctxy->tbc", prod_re, target_im, precision=high) - jnp.einsum(
        "btxy,ctxy->tbc", prod_im, target_re, precision=high
    )
    return (jnp.stack([cross_re, cross_im], axis=1), target_re, target_im)


def leading(matrices):
    high = lax.Precision.HIGHEST
    mat_re = matrices[:, 0]
    mat_im = matrices[:, 1]
    vec_re = jnp.full(mat_re.shape[:2], 1.0 / math.sqrt(mat_re.shape[1]), jnp.float32)
    vec_im = jnp.zeros(mat_re.shape[:2], jnp.float32)

    def apply(part_re, part_im):
        out_re = jnp.einsum("tbc,tc->tb", mat_re, part_re, precision=high) - jnp.einsum(
            "tbc,tc->tb", mat_im, part_im, precision=high
        )
        out_im = jnp.einsum("tbc,tc->tb", mat_re, part_im, precision=high) + jnp.einsum(
            "tbc,tc->tb", mat_im, part_re, precision=high
        )
        return (out_re, out_im)

    for repeat in range(POW):
        out_re, out_im = apply(vec_re, vec_im)
        length = jnp.sqrt(jnp.sum(out_re * out_re + out_im * out_im, axis=1, keepdims=True))
        vec_re = out_re / length
        vec_im = out_im / length
    out_re, out_im = apply(vec_re, vec_im)
    value_re = jnp.sum(vec_re * out_re + vec_im * out_im, axis=1)
    value_im = jnp.sum(vec_re * out_im - vec_im * out_re, axis=1)
    return (jnp.stack([vec_re, vec_im], axis=1), jnp.stack([value_re, value_im], axis=1))


def on_device(u_velocity, v_velocity, cell_weights, block_offsets, triads):
    u_part = with_halo(u_velocity, (("freq", 2),), 1).astype(jnp.float32)
    v_part = with_halo(v_velocity, (("space", 1),), 1).astype(jnp.float32)
    vorticity = 0.5 * (v_part[:, 2:, :] - v_part[:, :-2, :]) - 0.5 * (
        u_part[:, :, 2:] - u_part[:, :, :-2]
    )
    spectrum = spectra(vorticity, block_offsets)
    partial_value, target_re, target_im = cross_terms(spectrum, cell_weights, triads)
    cells = vorticity.shape[1] * vorticity.shape[2] * lax.axis_size("space") * lax.axis_size("freq")
    scaling = 1.0 / (partial_value.shape[2] * math.sqrt(cells))
    mine = lax.psum_scatter(partial_value, "freq", scatter_dimension=0, tiled=True)
    mine = lax.psum(mine, "space") * scaling
    own_vectors, own_values = leading(mine)
    vectors, values = (
        lax.all_gather(own_vectors, "freq", axis=0, tiled=True),
        lax.all_gather(own_values, "freq", axis=0, tiled=True),
    )
    high = lax.Precision.HIGHEST
    vec_re = vectors[:, 0]
    vec_im = vectors[:, 1]
    mode_re = jnp.einsum("tb,btxy->txy", vec_re, target_re, precision=high) - jnp.einsum(
        "tb,btxy->txy", vec_im, target_im, precision=high
    )
    mode_im = jnp.einsum("tb,btxy->txy", vec_re, target_im, precision=high) + jnp.einsum(
        "tb,btxy->txy", vec_im, target_re, precision=high
    )
    return (values, jnp.stack([mode_re, mode_im], axis=1))


def solution(mesh):
    return jax.shard_map(
        on_device,
        mesh=mesh,
        in_specs=(P(None, "space", "freq"), P(None, "space", "freq"), P("space", "freq"), P(), P()),
        out_specs=(P(), P(None, None, "space", "freq")),
        check_vma=False,
    )
```

profile of v0, /device:TPU:0, one launch (start us, length us, event | category | flops | bytes accessed | tf_op | source)
XLA Modules:
  0.0 192.5 jit_solution(13298839978467539383)
XLA Ops:
  7.2 3.7 %fusion.92 = (bf16[2176,1,128]{2,1,0:T(2,128)(2,1)S(1)}, bf16[2176,1,128]{2,1,0:T(2,128)(2,1)S(1)}) fusion(bf16[2176,2,128]{2,1,0:T(2,128)(2,1)} %param.8), kind=kLoop, calls=%fused_computation.155 | loop fusion | bytes 2228224 | tf_op jit(solution)/shard_map/slice | solution.py:16
  10.9 0.9 copy.121
  11.8 5.7 %collective-permute-start = (bf16[2176,1,128]{2,0,1:T(8,128)(2,1)}, bf16[2176,1,128]{2,0,1:T(8,128)(2,1)}, u32[]{:S(2)}, u32[]{:S(2)}) collective-permute-start(bf16[2176,1,128]{2,0,1:T(8,128)(2,1)} %copy.121), channel_id=1, source_target_pairs={{0,4},{4,8},{8,12},{12,16},{16,20},{20,24},{24,28},{1,5},{5,9},{9,... | collective-permute-start | bytes 1671176 | tf_op jit(solution)/shard_map/ppermute | solution.py:19
  17.5 0.9 copy.122
  18.4 1.3 collective-permute-start.1
  19.7 2.1 %fusion.93 = (bf16[2176,2,1]{2,1,0:T(2,128)(2,1)S(1)}, bf16[2176,2,1]{2,1,0:T(2,128)(2,1)S(1)}) fusion(bf16[2176,2,128]{2,1,0:T(2,128)(2,1)S(1)} %copy-done.2), kind=kLoop, calls=%fused_computation.156 | loop fusion | bytes 34816 | tf_op jit(solution)/shard_map/slice | solution.py:16
  21.8 1.3 copy.123
  23.1 1.5 collective-permute-start.2
  24.6 1.3 copy.124
  25.9 1.5 collective-permute-start.3
  27.4 0.6 multiply_reduce_fusion
  28.7 0.5 multiply_convert_fusion
  29.4 1.6 copy.66
  31.0 1.6 copy.67
  32.7 6.0 %maximum_convert_fusion.1 = f32[2176,2,130]{2,1,0:T(2,128)S(1)} fusion(bf16[2176,2,1]{2,1,0:T(2,128)(2,1)S(1)} %copy.67, bf16[2176,2,128]{2,1,0:T(2,128)(2,1)S(1)} %copy-done.2, bf16[2176,2,1]{2,1,0:T(2,128)(2,1)S(1)} %copy.66), kind=kLoop, calls=%fused_computation.15 | loop fusion | flops 3394560 | bytes 3394560 | tf_op jit(solution)/shard_map/convert_element_type | solution.py:99
  38.7 2.1 %collective-permute-done = bf16[2176,1,128]{2,0,1:T(8,128)(2,1)} collective-permute-done((bf16[2176,1,128]{2,0,1:T(8,128)(2,1)}, bf16[2176,1,128]{2,0,1:T(8,128)(2,1)}, u32[]{:S(2)}, u32[]{:S(2)}) %collective-permute-start) | collective-permute-done | bytes 557088 | tf_op jit(solution)/shard_map/ppermute | solution.py:19
  40.8 5.6 %copy.62 = bf16[2176,1,128]{2,1,0:T(2,128)(2,1)S(1)} copy(bf16[2176,1,128]{2,0,1:T(8,128)(2,1)} %collective-permute-done) | data formatting | bytes 1114112 | tf_op jit(solution)/shard_map/ppermute | solution.py:19
  46.4 5.6 %copy.63 = bf16[2176,1,128]{2,1,0:T(2,128)(2,1)S(1)} copy(bf16[2176,1,128]{2,0,1:T(8,128)(2,1)} %collective-permute-done.1) | data formatting | bytes 1114112 | tf_op jit(solution)/shard_map/ppermute | solution.py:21
  52.0 3.5 %maximum_convert_fusion = f32[2176,4,128]{2,1,0:T(4,128)S(1)} fusion(bf16[2176,1,128]{2,1,0:T(2,128)(2,1)S(1)} %copy.63, bf16[2176,2,128]{2,1,0:T(2,128)(2,1)S(1)} %copy-done.3, bf16[2176,1,128]{2,1,0:T(2,128)(2,1)S(1)} %copy.62), kind=kLoop, calls=%fused_computation.14 | loop fusion | flops 6684672 | bytes 6684672 | tf_op jit(solution)/shard_map/convert_element_type | solution.py:100
  55.6 3.1 %fusion.89 = (f32[2,128]{1,0:T(2,128)S(1)}, f32[2176,2,128]{2,1,0:T(2,128)S(1)}) fusion(f32[2176,2,130]{2,1,0:T(2,128)S(1)} %maximum_convert_fusion.1, f32[2176,4,128]{2,1,0:T(4,128)S(1)} %maximum_convert_fusion), kind=kLoop, calls=%fused_computation.153 | loop fusion | flops 3342080 | bytes 11142144 | tf_op jit(solution)/shard_map/reduce_sum | solution.py:42
  58.9 6.5 %gather_fusion = f32[16,256,2,128]{3,2,1,0:T(2,128)} fusion(f32[2176,2,128]{2,1,0:T(2,128)S(1)} %bitcast.240, s32[16]{0:T(128)S(1)} %fusion.79), kind=kCustom, calls=%fused_computation.6 | custom fusion | bytes 8388800 | tf_op jit(solution)/shard_map/vmap()/gather | solution.py:43
  65.3 3.0 %convolution_bitcast_fusion = f32[16,256,2,128]{1,3,2,0:T(8,128)S(1)} fusion(f32[16,256,2,128]{3,2,1,0:T(2,128)} %gather_fusion, f32[256]{0:T(256)S(1)} %multiply_subtract_fusion, bf16[128,256]{1,0:T(8,128)(2,1)S(1)} %get-tuple-element.47, bf16[128,256]{1,0:T(8,128)(2,1)S(1)} %get-tuple-element.48), kind=kOutput, calls=%fused_computation.16 | convolution fusion | flops 539230208 | bytes 8520704 | tf_op jit(solution)/shard_map/ft,btxy->bfxy/dot_general | solution.py:45
  68.4 2.5 %fusion.91 = (f32[16,128,2,128]{1,3,2,0:T(8,128)}, f32[16,128,2,128]{1,3,2,0:T(8,128)}) fusion(f32[16,256,2,128]{1,3,2,0:T(8,128)S(1)} %convolution_bitcast_fusion), kind=kLoop, calls=%fused_computation.154 | loop fusion | bytes 8388608 | tf_op jit(solution)/shard_map/slice | solution.py:50
  70.9 2.4 %copy.70 = f32[16,128,2,128]{3,0,2,1:T(8,128)S(1)} copy(f32[16,128,2,128]{1,3,2,0:T(8,128)} %get-tuple-element.27) | data formatting | bytes 4194304 | tf_op jit(solution)/shard_map/slice | solution.py:50
  73.3 3.9 %copy.72 = f32[16,128,2,128]{3,0,2,1:T(8,128)} copy(f32[16,128,2,128]{1,3,2,0:T(8,128)} %get-tuple-element.28) | data formatting | bytes 4194304 | tf_op jit(solution)/shard_map/slice | solution.py:51
  77.1 1.6 gather_fusion.2
  78.8 3.2 %gather_fusion.4 = f32[64,16,2,128]{3,1,2,0:T(8,128)} fusion(f32[16,128,2,128]{3,0,2,1:T(8,128)} %copy.72, s32[1024]{0:T(1024)S(1)} %get-tuple-element.50), kind=kCustom, calls=%fused_computation.3.clone | custom fusion | bytes 2097408 | tf_op jit(solution)/shard_map/jit(_take)/gather | solution.py:56
  82.0 1.6 gather_fusion.1
  83.6 3.3 %gather_fusion.3 = f32[64,16,2,128]{3,1,2,0:T(8,128)} fusion(f32[16,128,2,128]{3,0,2,1:T(8,128)} %copy.72, s32[1024]{0:T(1024)S(1)} %pad_clamp_fusion.2), kind=kCustom, calls=%fused_computation.2.clone | custom fusion | bytes 2097408 | tf_op jit(solution)/shard_map/jit(_take)/gather | solution.py:54
  86.9 0.6 gather_fusion.6
  87.6 2.3 %gather_fusion.5 = f32[64,16,2,128]{3,1,2,0:T(8,128)S(1)} fusion(f32[16,128,2,128]{3,0,2,1:T(8,128)} %copy-done, s32[1024]{0:T(1024)S(1)} %get-tuple-element.49), kind=kCustom, calls=%fused_computation.4.clone | custom fusion | bytes 2097408 | tf_op jit(solution)/shard_map/jit(_take)/gather | solution.py:57
  89.9 2.4 %fusion.23 = (f32[16,64,2,128]{3,0,2,1:T(8,128)S(1)}, f32[16,64,2,128]{3,0,2,1:T(8,128)S(1)}) fusion(f32[64,16,2,128]{3,1,2,0:T(8,128)} %gather_fusion.4, f32[64,16,2,128]{3,1,2,0:T(8,128)} %gather_fusion.3, f32[64,16,2,128]{3,1,2,0:T(8,128)S(1)} %copy-done.4, f32[64,16,2,128]{3,1,2,0:T(8,128)} %gather_fusion.1, f32[2,128]{1,0:T(2,128)S(1)} %copy-done.5, ...), kind=kLoop, calls=%fused_computation.43 | loop fusion | flops 3145728 | bytes 6292608 | tf_op jit(solution)/shard_map/mul | solution.py:59
  92.3 1.2 convolution_bitcast_fusion.3
  93.4 1.2 convolution_bitcast_fusion.1
  94.6 1.2 fusion.7
  95.8 1.2 fusion.9
  97.2 1.3 reshape.159
  98.5 22.9 %reduce-scatter.4.cloned.1.call-done = f32[16,512]{1,0:T(8,128)} async-done(((f32[64,512]{1,0:T(8,128)}), f32[16,512]{1,0:T(8,128)}) %reduce-scatter.4.cloned.1.call-update) | async-done | bytes 32784
  121.5 0.9 reshape.160
  122.4 40.6 %psum.7 = f32[16,2,16,16]{3,2,0,1:T(8,128)S(1)} all-reduce(f32[16,2,16,16]{3,2,0,1:T(8,128)S(1)} %copy.120), channel_id=1, replica_groups=mesh['space'=8,'freq'=4] {'space'}, use_global_device_ids=true, to_apply=%region_3.5 | all-reduce | flops 8192 | bytes 65536 | tf_op jit(solution)/shard_map/psum | solution.py:109
  163.4 0.3 fusion.66
  164.0 0.3 fusion.67
  164.6 0.3 fusion.64
  164.9 0.3 fusion.75
  165.3 0.3 fusion.74
  165.6 0.3 fusion.65
  166.1 0.3 fusion.62
  166.5 0.3 fusion.73
  166.8 0.3 fusion.72
  167.1 0.3 fusion.63
  167.7 0.3 fusion.60
  168.0 0.3 fusion.71
  168.3 0.3 fusion.70
  168.7 0.3 fusion.61
  169.2 5.2 %all_gather.7 = f32[64,2,16]{2,0,1:T(8,128)S(1)} all-gather(f32[16,2,16]{2,0,1:T(8,128)S(1)} %pad_maximum_fusion.2), channel_id=1, replica_groups=mesh['space'=8,'freq'=4] {'freq'}, dimensions={0}, use_global_device_ids=true | all-gather | bytes 10240 | tf_op jit(solution)/shard_map/all_gather | solution.py:112
  174.5 0.8 fusion.12
  175.3 0.8 fusion.16
  176.1 0.8 fusion.18
  176.9 0.8 fusion.10
  178.4 0.3 fusion.69
  178.7 0.3 fusion.58
  179.1 5.1 %all-gather = f32[4,16,2]{1,2,0:T(2,128)S(1)} all-gather(f32[1,16,2]{1,2,0:T(2,128)S(1)} %maximum_bitcast_fusion.2), channel_id=1, replica_groups=mesh['space'=8,'freq'=4] {'freq'}, dimensions={0}, use_global_device_ids=true | all-gather | bytes 640 | tf_op jit(solution)/shard_map/all_gather | solution.py:113
  184.2 0.6 reshape.105
  185.0 0.7 pad_maximum_fusion.1
  (58 shorter events, 2.9 us)
Async XLA Ops:
  7.2 114.3 %reduce-scatter.4.cloned.1.call-start = ((), (), s32[]{:S(2)}) async-start(), calls=%async_computation.1 | async-start | bytes 163840
  10.9 8.8 %copy-start.2 = (bf16[2176,2,128]{2,1,0:T(2,128)(2,1)S(1)}, bf16[2176,2,128]{2,1,0:T(2,128)(2,1)}, u32[]{:S(2)}) copy-start(bf16[2176,2,128]{2,1,0:T(2,128)(2,1)} %param.7) | copy-start | bytes 3342340
  11.8 29.0 %collective-permute-start = (bf16[2176,1,128]{2,0,1:T(8,128)(2,1)}, bf16[2176,1,128]{2,0,1:T(8,128)(2,1)}, u32[]{:S(2)}, u32[]{:S(2)}) collective-permute-start(bf16[2176,1,128]{2,0,1:T(8,128)(2,1)} %copy.121), channel_id=1, source_target_pairs={{0,4},{4,8},{8,12},{12,16},{16,20},{20,24},{24,28},{1,5},{5,9},{9,... | collective-permute-start | bytes 1671176 | tf_op jit(solution)/shard_map/ppermute | solution.py:19
  18.4 28.0 %collective-permute-start.1 = (bf16[2176,1,128]{2,0,1:T(8,128)(2,1)}, bf16[2176,1,128]{2,0,1:T(8,128)(2,1)}, u32[]{:S(2)}, u32[]{:S(2)}) collective-permute-start(bf16[2176,1,128]{2,0,1:T(8,128)(2,1)} %copy.122), channel_id=1, source_target_pairs={{4,0},{8,4},{12,8},{16,12},{20,16},{24,20},{28,24},{5,1},{9,5},{13... | collective-permute-start | bytes 1671176 | tf_op jit(solution)/shard_map/ppermute | solution.py:21
  21.8 6.3 %copy-start.7 = (s32[16]{0:T(128)S(1)}, s32[16]{0:T(128)}, u32[]{:S(2)}) copy-start(s32[16]{0:T(128)} %param.10) | copy-start | bytes 196
  21.8 7.5 %copy-start.6 = (s32[64,2]{0,1:T(2,128)S(1)}, s32[64,2]{0,1:T(2,128)}, u32[]{:S(2)}) copy-start(s32[64,2]{0,1:T(2,128)} %param.11) | copy-start | bytes 1540
  23.1 6.3 %collective-permute-start.2 = (bf16[2176,2,1]{0,1,2:T(2,128)(2,1)S(1)}, bf16[2176,2,1]{0,1,2:T(2,128)(2,1)S(1)}, u32[]{:S(2)}, u32[]{:S(2)}) collective-permute-start(bf16[2176,2,1]{0,1,2:T(2,128)(2,1)S(1)} %copy.123), channel_id=1, source_target_pairs={{0,1},{1,2},{2,3},{4,5},{5,6},{6,7},{8,9},{9,10},{10,11},{12,13},{... | collective-permute-start | bytes 26120 | tf_op jit(solution)/shard_map/ppermute | solution.py:19
  25.9 5.1 %collective-permute-start.3 = (bf16[2176,2,1]{0,1,2:T(2,128)(2,1)S(1)}, bf16[2176,2,1]{0,1,2:T(2,128)(2,1)S(1)}, u32[]{:S(2)}, u32[]{:S(2)}) collective-permute-start(bf16[2176,2,1]{0,1,2:T(2,128)(2,1)S(1)} %copy.124), channel_id=1, source_target_pairs={{1,0},{2,1},{3,2},{5,4},{6,5},{7,6},{9,8},{10,9},{11,10},{13,12},{... | collective-permute-start | bytes 26120 | tf_op jit(solution)/shard_map/ppermute | solution.py:21
  38.7 13.3 %copy-start.3 = (bf16[2176,2,128]{2,1,0:T(2,128)(2,1)S(1)}, bf16[2176,2,128]{2,1,0:T(2,128)(2,1)}, u32[]{:S(2)}) copy-start(bf16[2176,2,128]{2,1,0:T(2,128)(2,1)} %param.8) | copy-start | bytes 3342340
  73.3 8.7 %copy-start = (f32[16,128,2,128]{3,0,2,1:T(8,128)}, f32[16,128,2,128]{3,0,2,1:T(8,128)S(1)}, u32[]{:S(2)}) copy-start(f32[16,128,2,128]{3,0,2,1:T(8,128)S(1)} %copy.70) | copy-start | bytes 6291460
  83.6 3.4 %copy-start.1 = (f32[16,128,2,128]{3,0,2,1:T(8,128)S(1)}, f32[16,128,2,128]{3,0,2,1:T(8,128)}, u32[]{:S(2)}) copy-start(f32[16,128,2,128]{3,0,2,1:T(8,128)} %copy.72) | copy-start | bytes 6291460
  86.9 3.0 %copy-start.5 = (f32[2,128]{1,0:T(2,128)S(1)}, f32[2,128]{1,0:T(2,128)}, u32[]{:S(2)}) copy-start(f32[2,128]{1,0:T(2,128)} %param.9) | copy-start | bytes 3076
  87.6 2.3 %copy-start.4 = (f32[64,16,2,128]{3,1,2,0:T(8,128)S(1)}, f32[64,16,2,128]{3,1,2,0:T(8,128)}, u32[]{:S(2)}) copy-start(f32[64,16,2,128]{3,1,2,0:T(8,128)} %gather_fusion.2) | copy-start | bytes 3145732
Sparse Core Ops, SparseCore 0:
  98.6 22.7 reduce-scatter.3
where the time goes:
time: 193 us
  local copies, waits for them, and re-layouts  55.6 us (29%)
  blocking collectives  50.9 us (26%)
  waiting for transfers between devices  25.1 us (13%)
  other arithmetic  18.2 us (9%)
  matrix products  17.5 us (9%)
  between operations  15.3 us (8%)
  starting transfers between devices  9.92 us (5%)
    psum x1, blocking collectives, on_device(): mine = lax.psum(mine, 'space') * scaling  40.6 us
    unnamed x2, waiting for transfers between devices  23 us
    unnamed x26, local copies, waits for them, and re-layouts  7.42 us
    ppermute x2, local copies, waits for them, and re-layouts, with_halo(): lax.ppermute(head, axis, [((i + 1) % count, i) for i in range(ends)])  7.22 us
    ppermute x2, local copies, waits for them, and re-layouts, with_halo(): lax.ppermute(tail, axis, [(i, (i + 1) % count) for i in range(ends)])  7.22 us
    ppermute x2, starting transfers between devices, with_halo(): lax.ppermute(tail, axis, [(i, (i + 1) % count) for i in range(ends)])  7.13 us
    gather x1, local copies, waits for them, and re-layouts, spectra(): lax.dynamic_slice_in_dim(fluct, start, NFFT, 0)  6.47 us
    convert_element_type x1, other arithmetic, on_device(): u_part = with_halo(u_velocity, (('freq', 2),), 1).astype(jnp.float32)  5.99 us
  transfers between devices with their start and end apart: 5, of which 2 were waited for; matrix products, arithmetic and copies ran while one was open for 11% of the time, Pallas kernels for 0%

commit v1 on v0

--- a/solution.py
+++ b/solution.py
@@ -6,6 +6,11 @@
 
 NFFT = 256
 POW = 4
+
+
+def summed_here(block, axis):
+    terms = lax.all_gather(block, axis)
+    return jnp.sum(terms, axis=0)
 
 
 def with_halo(cells, sides, width):
@@ -106,7 +111,7 @@
     cells = vorticity.shape[1] * vorticity.shape[2] * lax.axis_size("space") * lax.axis_size("freq")
     scaling = 1.0 / (partial_value.shape[2] * math.sqrt(cells))
     mine = lax.psum_scatter(partial_value, "freq", scatter_dimension=0, tiled=True)
-    mine = lax.psum(mine, "space") * scaling
+    mine = summed_here(mine, "space") * scaling
     own_vectors, own_values = leading(mine)
     vectors, values = (
         lax.all_gather(own_vectors, "freq", axis=0, tiled=True),

time: 193 us -> 200 us (1.036)
  blocking collectives: 50.9 us -> 55.7 us
    all_gather x0 -> x1, blocking collectives: none -> 45.4 us  [summed_here(): terms = lax.all_gather(block, axis)]
    psum x1 -> x0, blocking collectives: 40.6 us -> none  [on_device(): mine = lax.psum(mine, 'space') * scaling]
    unnamed x26 -> x22, local copies, waits for them, and re-layouts: 7.42 us -> 7.4 us
where the time goes in v1:
time: 200 us; the launch traced here: 199 us
  local copies, waits for them, and re-layouts  55.9 us (28%)
  blocking collectives  55.7 us (28%)
  waiting for transfers between devices  25.1 us (13%)
  other arithmetic  20 us (10%)
  matrix products  17.5 us (9%)
  between operations  15.3 us (8%)
  starting transfers between devices  9.91 us (5%)
    all_gather x1, blocking collectives, summed_here(): terms = lax.all_gather(block, axis)  45.4 us
    unnamed x2, waiting for transfers between devices  23 us
    unnamed x22, local copies, waits for them, and re-layouts  7.4 us
    ppermute x2, local copies, waits for them, and re-layouts, with_halo(): lax.ppermute(head, axis, [((i + 1) % count, i) for i in range(ends)])  7.22 us
    ppermute x2, local copies, waits for them, and re-layouts, with_halo(): lax.ppermute(tail, axis, [(i, (i + 1) % count) for i in range(ends)])  7.22 us
    ppermute x2, starting transfers between devices, with_halo(): lax.ppermute(tail, axis, [(i, (i + 1) % count) for i in range(ends)])  7.12 us
    gather x1, local copies, waits for them, and re-layouts, spectra(): lax.dynamic_slice_in_dim(fluct, start, NFFT, 0)  6.46 us
    convert_element_type x1, other arithmetic, on_device(): u_part = with_halo(u_velocity, (('freq', 2),), 1).astype(jnp.float32)  5.99 us
  transfers between devices with their start and end apart: 5, of which 2 were waited for; matrix products, arithmetic and copies ran while one was open for 11% of the time, Pallas kernels for 0%

profile of v1, /device:TPU:0, one launch (start us, length us, event | category | flops | bytes accessed | tf_op | source)
XLA Modules:
  0.0 199.3 jit_solution(6470622125032625136)
XLA Ops:
  7.2 3.7 %fusion.92 = (bf16[2176,1,128]{2,1,0:T(2,128)(2,1)S(1)}, bf16[2176,1,128]{2,1,0:T(2,128)(2,1)S(1)}) fusion(bf16[2176,2,128]{2,1,0:T(2,128)(2,1)} %param.8), kind=kLoop, calls=%fused_computation.155 | loop fusion | bytes 2228224 | tf_op jit(solution)/shard_map/slice | solution.py:21
  10.9 0.9 copy.121
  11.8 5.7 %collective-permute-start = (bf16[2176,1,128]{2,0,1:T(8,128)(2,1)}, bf16[2176,1,128]{2,0,1:T(8,128)(2,1)}, u32[]{:S(2)}, u32[]{:S(2)}) collective-permute-start(bf16[2176,1,128]{2,0,1:T(8,128)(2,1)} %copy.121), channel_id=1, source_target_pairs={{0,4},{4,8},{8,12},{12,16},{16,20},{20,24},{24,28},{1,5},{5,9},{9,... | collective-permute-start | bytes 1671176 | tf_op jit(solution)/shard_map/ppermute | solution.py:24
  17.5 0.9 copy.122
  18.4 1.3 collective-permute-start.1
  19.7 2.1 %fusion.93 = (bf16[2176,2,1]{2,1,0:T(2,128)(2,1)S(1)}, bf16[2176,2,1]{2,1,0:T(2,128)(2,1)S(1)}) fusion(bf16[2176,2,128]{2,1,0:T(2,128)(2,1)S(1)} %copy-done.1), kind=kLoop, calls=%fused_computation.156 | loop fusion | bytes 34816 | tf_op jit(solution)/shard_map/slice | solution.py:21
  21.8 1.3 copy.123
  23.1 1.5 collective-permute-start.2
  24.6 1.3 copy.124
  25.9 1.5 collective-permute-start.3
  27.4 0.6 multiply_reduce_fusion
  28.7 0.5 multiply_convert_fusion
  29.4 1.6 copy.66
  31.0 1.6 copy.67
  32.7 6.0 %maximum_convert_fusion.1 = f32[2176,2,130]{2,1,0:T(2,128)S(1)} fusion(bf16[2176,2,1]{2,1,0:T(2,128)(2,1)S(1)} %copy.67, bf16[2176,2,128]{2,1,0:T(2,128)(2,1)S(1)} %copy-done.1, bf16[2176,2,1]{2,1,0:T(2,128)(2,1)S(1)} %copy.66), kind=kLoop, calls=%fused_computation.15 | loop fusion | flops 3394560 | bytes 3394560 | tf_op jit(solution)/shard_map/convert_element_type | solution.py:104
  38.7 2.1 %collective-permute-done = bf16[2176,1,128]{2,0,1:T(8,128)(2,1)} collective-permute-done((bf16[2176,1,128]{2,0,1:T(8,128)(2,1)}, bf16[2176,1,128]{2,0,1:T(8,128)(2,1)}, u32[]{:S(2)}, u32[]{:S(2)}) %collective-permute-start) | collective-permute-done | bytes 557088 | tf_op jit(solution)/shard_map/ppermute | solution.py:24
  40.8 5.6 %copy.62 = bf16[2176,1,128]{2,1,0:T(2,128)(2,1)S(1)} copy(bf16[2176,1,128]{2,0,1:T(8,128)(2,1)} %collective-permute-done) | data formatting | bytes 1114112 | tf_op jit(solution)/shard_map/ppermute | solution.py:24
  46.4 5.6 %copy.63 = bf16[2176,1,128]{2,1,0:T(2,128)(2,1)S(1)} copy(bf16[2176,1,128]{2,0,1:T(8,128)(2,1)} %collective-permute-done.1) | data formatting | bytes 1114112 | tf_op jit(solution)/shard_map/ppermute | solution.py:26
  52.0 3.5 %maximum_convert_fusion = f32[2176,4,128]{2,1,0:T(4,128)S(1)} fusion(bf16[2176,1,128]{2,1,0:T(2,128)(2,1)S(1)} %copy.63, bf16[2176,2,128]{2,1,0:T(2,128)(2,1)S(1)} %copy-done.2, bf16[2176,1,128]{2,1,0:T(2,128)(2,1)S(1)} %copy.62), kind=kLoop, calls=%fused_computation.14 | loop fusion | flops 6684672 | bytes 6684672 | tf_op jit(solution)/shard_map/convert_element_type | solution.py:105
  55.6 3.1 %fusion.89 = (f32[2,128]{1,0:T(2,128)S(1)}, f32[2176,2,128]{2,1,0:T(2,128)S(1)}) fusion(f32[2176,2,130]{2,1,0:T(2,128)S(1)} %maximum_convert_fusion.1, f32[2176,4,128]{2,1,0:T(4,128)S(1)} %maximum_convert_fusion), kind=kLoop, calls=%fused_computation.153 | loop fusion | flops 3342080 | bytes 11142144 | tf_op jit(solution)/shard_map/reduce_sum | solution.py:47
  58.9 6.5 %gather_fusion = f32[16,256,2,128]{3,2,1,0:T(2,128)} fusion(f32[2176,2,128]{2,1,0:T(2,128)S(1)} %bitcast.241, s32[16]{0:T(128)S(1)} %fusion.79), kind=kCustom, calls=%fused_computation.6 | custom fusion | bytes 8388800 | tf_op jit(solution)/shard_map/vmap()/gather | solution.py:48
  65.3 3.0 %convolution_bitcast_fusion = f32[16,256,2,128]{1,3,2,0:T(8,128)S(1)} fusion(f32[16,256,2,128]{3,2,1,0:T(2,128)} %gather_fusion, f32[256]{0:T(256)S(1)} %multiply_subtract_fusion, bf16[128,256]{1,0:T(8,128)(2,1)S(1)} %get-tuple-element.47, bf16[128,256]{1,0:T(8,128)(2,1)S(1)} %get-tuple-element.48), kind=kOutput, calls=%fused_computation.16 | convolution fusion | flops 539230208 | bytes 8520704 | tf_op jit(solution)/shard_map/ft,btxy->bfxy/dot_general | solution.py:50
  68.3 2.5 %fusion.91 = (f32[16,128,2,128]{1,3,2,0:T(8,128)}, f32[16,128,2,128]{1,3,2,0:T(8,128)}) fusion(f32[16,256,2,128]{1,3,2,0:T(8,128)S(1)} %convolution_bitcast_fusion), kind=kLoop, calls=%fused_computation.154 | loop fusion | bytes 8388608 | tf_op jit(solution)/shard_map/slice | solution.py:55
  70.9 2.4 %copy.70 = f32[16,128,2,128]{3,0,2,1:T(8,128)S(1)} copy(f32[16,128,2,128]{1,3,2,0:T(8,128)} %get-tuple-element.27) | data formatting | bytes 4194304 | tf_op jit(solution)/shard_map/slice | solution.py:55
  73.3 3.9 %copy.72 = f32[16,128,2,128]{3,0,2,1:T(8,128)} copy(f32[16,128,2,128]{1,3,2,0:T(8,128)} %get-tuple-element.28) | data formatting | bytes 4194304 | tf_op jit(solution)/shard_map/slice | solution.py:56
  77.1 0.6 gather_fusion.2
  77.8 3.2 %gather_fusion.4 = f32[64,16,2,128]{3,1,2,0:T(8,128)} fusion(f32[16,128,2,128]{3,0,2,1:T(8,128)} %copy.72, s32[1024]{0:T(1024)S(1)} %get-tuple-element.50), kind=kCustom, calls=%fused_computation.3.clone | custom fusion | bytes 2097408 | tf_op jit(solution)/shard_map/jit(_take)/gather | solution.py:61
  80.9 1.6 gather_fusion.1
  82.6 3.2 %gather_fusion.3 = f32[64,16,2,128]{3,1,2,0:T(8,128)} fusion(f32[16,128,2,128]{3,0,2,1:T(8,128)} %copy.72, s32[1024]{0:T(1024)S(1)} %pad_clamp_fusion.2), kind=kCustom, calls=%fused_computation.2.clone | custom fusion | bytes 2097408 | tf_op jit(solution)/shard_map/jit(_take)/gather | solution.py:59
  85.8 2.2 %gather_fusion.6 = f32[64,16,2,128]{3,1,2,0:T(8,128)S(1)} fusion(f32[16,128,2,128]{3,0,2,1:T(8,128)} %copy.72, s32[1024]{0:T(1024)S(1)} %get-tuple-element.49), kind=kCustom, calls=%fused_computation.5.clone | custom fusion | bytes 2097408 | tf_op jit(solution)/shard_map/jit(_take)/gather | solution.py:63
  88.0 2.2 %gather_fusion.5 = f32[64,16,2,128]{3,1,2,0:T(8,128)S(1)} fusion(f32[16,128,2,128]{3,0,2,1:T(8,128)} %copy-done, s32[1024]{0:T(1024)S(1)} %get-tuple-element.49), kind=kCustom, calls=%fused_computation.4.clone | custom fusion | bytes 2097408 | tf_op jit(solution)/shard_map/jit(_take)/gather | solution.py:62
  90.2 2.4 %fusion.23 = (f32[16,64,2,128]{3,0,2,1:T(8,128)S(1)}, f32[16,64,2,128]{3,0,2,1:T(8,128)S(1)}) fusion(f32[64,16,2,128]{3,1,2,0:T(8,128)} %gather_fusion.4, f32[64,16,2,128]{3,1,2,0:T(8,128)} %gather_fusion.3, f32[64,16,2,128]{3,1,2,0:T(8,128)S(1)} %gather_fusion.2, f32[64,16,2,128]{3,1,2,0:T(8,128)} %gather_fusion.1, f32[2,128]{1,0:T(2,128)S(1)} %copy-done.3, ...), kind=kLoop, calls=%fused_computation.43 | loop fusion | flops 3145728 | bytes 6292608 | tf_op jit(solution)/shard_map/mul | solution.py:64
  92.6 1.2 convolution_bitcast_fusion.3
  93.8 1.2 convolution_bitcast_fusion.1
  94.9 1.2 fusion.7
  96.1 1.2 fusion.9
  97.5 1.3 reshape.160
  98.8 22.9 %reduce-scatter.4.cloned.1.call-done = f32[16,512]{1,0:T(8,128)} async-done(((f32[64,512]{1,0:T(8,128)}), f32[16,512]{1,0:T(8,128)}) %reduce-scatter.4.cloned.1.call-update) | async-done | bytes 32784
  121.8 0.9 reshape.161
  122.7 45.4 %all-gather = f32[128,2,16,16]{3,2,0,1:T(8,128)} all-gather(f32[16,2,16,16]{3,2,0,1:T(8,128)S(1)} %copy.120), channel_id=2, replica_groups=mesh['space'=8,'freq'=4] {'space'}, dimensions={0}, use_global_device_ids=true | all-gather | bytes 294912 | tf_op jit(solution)/shard_map/all_gather | solution.py:12
  168.1 1.8 reduce_sum.83
  170.2 0.3 fusion.66
  170.9 0.3 fusion.67
  171.4 0.3 fusion.64
  171.8 0.3 fusion.75
  172.1 0.3 fusion.74
  172.4 0.3 fusion.65
  173.0 0.3 fusion.62
  173.3 0.3 fusion.73
  173.6 0.3 fusion.72
  174.0 0.3 fusion.63
  174.5 0.3 fusion.60
  174.8 0.3 fusion.71
  175.2 0.3 fusion.70
  176.1 5.2 %all_gather.15 = f32[64,2,16]{2,0,1:T(8,128)S(1)} all-gather(f32[16,2,16]{2,0,1:T(8,128)S(1)} %pad_maximum_fusion.2), channel_id=1, replica_groups=mesh['space'=8,'freq'=4] {'freq'}, dimensions={0}, use_global_device_ids=true | all-gather | bytes 10240 | tf_op jit(solution)/shard_map/all_gather | solution.py:117
  181.3 0.8 fusion.12
  182.1 0.8 fusion.16
  182.9 0.8 fusion.18
  183.7 0.8 fusion.10
  185.2 0.3 fusion.69
  185.5 0.3 fusion.58
  186.0 5.1 %all-gather.1 = f32[4,16,2]{1,2,0:T(2,128)S(1)} all-gather(f32[1,16,2]{1,2,0:T(2,128)S(1)} %maximum_bitcast_fusion.2), channel_id=1, replica_groups=mesh['space'=8,'freq'=4] {'freq'}, dimensions={0}, use_global_device_ids=true | all-gather | bytes 640 | tf_op jit(solution)/shard_map/all_gather | solution.py:118
  191.1 0.6 reshape.106
  191.8 0.7 pad_maximum_fusion.1
  (55 shorter events, 3.2 us)
Async XLA Ops:
  7.2 114.6 %reduce-scatter.4.cloned.1.call-start = ((), (), s32[]{:S(2)}) async-start(), calls=%async_computation.1 | async-start | bytes 163840
  10.9 8.7 %copy-start.1 = (bf16[2176,2,128]{2,1,0:T(2,128)(2,1)S(1)}, bf16[2176,2,128]{2,1,0:T(2,128)(2,1)}, u32[]{:S(2)}) copy-start(bf16[2176,2,128]{2,1,0:T(2,128)(2,1)} %param.7) | copy-start | bytes 3342340
  11.8 29.0 %collective-permute-start = (bf16[2176,1,128]{2,0,1:T(8,128)(2,1)}, bf16[2176,1,128]{2,0,1:T(8,128)(2,1)}, u32[]{:S(2)}, u32[]{:S(2)}) collective-permute-start(bf16[2176,1,128]{2,0,1:T(8,128)(2,1)} %copy.121), channel_id=1, source_target_pairs={{0,4},{4,8},{8,12},{12,16},{16,20},{20,24},{24,28},{1,5},{5,9},{9,... | collective-permute-start | bytes 1671176 | tf_op jit(solution)/shard_map/ppermute | solution.py:24
  18.4 28.0 %collective-permute-start.1 = (bf16[2176,1,128]{2,0,1:T(8,128)(2,1)}, bf16[2176,1,128]{2,0,1:T(8,128)(2,1)}, u32[]{:S(2)}, u32[]{:S(2)}) collective-permute-start(bf16[2176,1,128]{2,0,1:T(8,128)(2,1)} %copy.122), channel_id=1, source_target_pairs={{4,0},{8,4},{12,8},{16,12},{20,16},{24,20},{28,24},{5,1},{9,5},{13... | collective-permute-start | bytes 1671176 | tf_op jit(solution)/shard_map/ppermute | solution.py:26
  21.8 6.3 %copy-start.5 = (s32[16]{0:T(128)S(1)}, s32[16]{0:T(128)}, u32[]{:S(2)}) copy-start(s32[16]{0:T(128)} %param.10) | copy-start | bytes 196
  21.8 7.5 %copy-start.4 = (s32[64,2]{0,1:T(2,128)S(1)}, s32[64,2]{0,1:T(2,128)}, u32[]{:S(2)}) copy-start(s32[64,2]{0,1:T(2,128)} %param.11) | copy-start | bytes 1540
  23.1 6.3 %collective-permute-start.2 = (bf16[2176,2,1]{0,1,2:T(2,128)(2,1)S(1)}, bf16[2176,2,1]{0,1,2:T(2,128)(2,1)S(1)}, u32[]{:S(2)}, u32[]{:S(2)}) collective-permute-start(bf16[2176,2,1]{0,1,2:T(2,128)(2,1)S(1)} %copy.123), channel_id=1, source_target_pairs={{0,1},{1,2},{2,3},{4,5},{5,6},{6,7},{8,9},{9,10},{10,11},{12,13},{... | collective-permute-start | bytes 26120 | tf_op jit(solution)/shard_map/ppermute | solution.py:24
  25.9 5.1 %collective-permute-start.3 = (bf16[2176,2,1]{0,1,2:T(2,128)(2,1)S(1)}, bf16[2176,2,1]{0,1,2:T(2,128)(2,1)S(1)}, u32[]{:S(2)}, u32[]{:S(2)}) collective-permute-start(bf16[2176,2,1]{0,1,2:T(2,128)(2,1)S(1)} %copy.124), channel_id=1, source_target_pairs={{1,0},{2,1},{3,2},{5,4},{6,5},{7,6},{9,8},{10,9},{11,10},{13,12},{... | collective-permute-start | bytes 26120 | tf_op jit(solution)/shard_map/ppermute | solution.py:26
  38.7 13.4 %copy-start.2 = (bf16[2176,2,128]{2,1,0:T(2,128)(2,1)S(1)}, bf16[2176,2,128]{2,1,0:T(2,128)(2,1)}, u32[]{:S(2)}) copy-start(bf16[2176,2,128]{2,1,0:T(2,128)(2,1)} %param.8) | copy-start | bytes 3342340
  73.3 7.7 %copy-start = (f32[16,128,2,128]{3,0,2,1:T(8,128)}, f32[16,128,2,128]{3,0,2,1:T(8,128)S(1)}, u32[]{:S(2)}) copy-start(f32[16,128,2,128]{3,0,2,1:T(8,128)S(1)} %copy.70) | copy-start | bytes 6291460
  85.8 4.4 %copy-start.3 = (f32[2,128]{1,0:T(2,128)S(1)}, f32[2,128]{1,0:T(2,128)}, u32[]{:S(2)}) copy-start(f32[2,128]{1,0:T(2,128)} %param.9) | copy-start | bytes 3076
Sparse Core Ops, SparseCore 0:
  99.0 22.7 reduce-scatter.3
